TPU v7x, 256 devices: a whole 4x4x8 slice. The times are simulated.
256 devices in a mesh: outer: 16 (over z_hi, x, core), inner: 16 (over z_lo, y).
Axes of the slice: x: 4, y: 4, z: 8 (z_hi: 2, z_lo: 4; z = z_hi * 4 + z_lo), core: 2. Of those that a mesh axis runs over, the one named last changes fastest.
Arguments:
- tokens: bfloat16 [65536, 2048], P(('outer', 'inner')), may hold values from -6 to 6
- w_qkv: bfloat16 [2048, 3072], P('inner'), may hold values from -2.8 to 2.8
- w_out: bfloat16 [1024, 2048], P(None, 'inner'), may hold values from -1.5 to 1.5
- neighbours: int32 [256, 5], P(('outer', 'inner')), may hold values from -1 to 255, as said below
- counts: int32 [256], replicated, may hold values from 1 to 256, as said below
Outputs:
- attended: bfloat16 [65536, 2048], P(('outer', 'inner'))
Inputs may be any that keep to these rules, and one draw needn't show every extreme that they name: `neighbours`: slot 0 of row b is b itself; slots 1 and 2 are the blocks b - 16 and b + 16 (the same inner index in the previous and next slab of outer), slots 3 and 4 the blocks b - 1 and b + 1 of the same slab; a slot holds -1 where its block lies outside the grid of blocks, and may hold -1 otherwise. `counts`: some block is full.
All inputs are finite; a program needn't handle non-finite values.
Results may differ from a plain program's by a relative error of at most 0.0093.
Values may be sent and summed in bfloat16 or wider, within the bound.
A program may use at most 64 MiB of HBM per device.

v0:
```python
import jax
import jax.numpy as jnp
from jax import lax
from jax.sharding import PartitionSpec as P

HD = 128


def padded(block, sides, width):
    for axis, dim in sides:
        count = lax.axis_size(axis)
        forward = [(i, i + 1) for i in range(count - 1)]
        backward = [(target, source) for source, target in forward]
        low = lax.ppermute(
            lax.slice_in_dim(block, block.shape[dim] - width, None, axis=dim), axis, forward
        )
        high = lax.ppermute(lax.slice_in_dim(block, 0, width, axis=dim), axis, backward)
        block = jnp.concatenate([low, block, high], axis=dim)
    return block


def normalize(values_in):
    values = values_in.astype(jnp.float32)
    center = values - jnp.mean(values, axis=-1, keepdims=True)
    spread = jnp.mean(center * center, axis=-1, keepdims=True)
    return (center * lax.rsqrt(spread + 1e-05)).astype(jnp.bfloat16)


def per_device(tokens, w_qkv, w_out, neighbours, counts):
    normed = normalize(tokens)
    rows_here = normed.shape[0]
    heads_all = w_out.shape[0]
    head_size = HD
    projected = jnp.dot(
        normed,
        lax.all_gather(w_qkv, "inner", axis=0, tiled=True),
        preferred_element_type=jnp.float32,
    ).astype(jnp.bfloat16)
    queries = projected[:, :heads_all]
    keys_values = projected[:, heads_all:]
    slab_halo = padded(keys_values[None], (("outer", 0),), 1)
    row_halo = padded(keys_values[None], (("inner", 0),), 1)
    candidates = (keys_values, slab_halo[0], slab_halo[2], row_halo[0], row_halo[2])
    listed = neighbours[0]
    clipped = jnp.maximum(listed, 0)
    block_ids = jnp.arange(counts.shape[0], dtype=jnp.int32)
    lengths = jnp.sum(jnp.where(clipped[:, None] == block_ids[None, :], counts[None, :], 0), axis=1)
    positions = jnp.arange(rows_here, dtype=jnp.int32)
    usable = (listed[:, None] >= 0) & (positions[None, :] < lengths[:, None])
    allowed = usable.reshape(-1)
    score_scale = float(head_size) ** (-0.5)
    outputs = []
    for head_index in range(heads_all // head_size):
        offset_q = head_index * head_size
        offset_v = heads_all + offset_q
        query_head = queries[:, offset_q : offset_q + head_size]
        scores = (
            jnp.concatenate(
                [
                    jnp.einsum(
                        "qd,kd->qk",
                        query_head,
                        source_kv[:, offset_q : offset_q + head_size],
                        preferred_element_type=jnp.float32,
                    )
                    for source_kv in candidates
                ],
                axis=1,
            )
            * score_scale
        )
        masked = jnp.where(allowed[None, :], scores, -jnp.inf)
        largest = jnp.max(masked, axis=1, keepdims=True)
        weights = jnp.exp(masked - largest)
        totals = jnp.sum(weights, axis=1, keepdims=True)
        rounded = weights.astype(jnp.bfloat16)
        context = jnp.zeros((rows_here, head_size), jnp.float32)
        for slot_no in range(len(candidates)):
            context = context + jnp.dot(
                rounded[:, slot_no * rows_here : (slot_no + 1) * rows_here],
                candidates[slot_no][:, offset_v : offset_v + head_size],
                preferred_element_type=jnp.float32,
            )
        outputs.append((context / totals).astype(jnp.bfloat16))
    context_all = jnp.concatenate(outputs, axis=1)
    return jnp.dot(
        context_all,
        lax.all_gather(w_out, "inner", axis=1, tiled=True),
        preferred_element_type=jnp.float32,
    ).astype(jnp.bfloat16)


def solution(mesh):
    placed = (
        P(("outer", "inner"), None),
        P("inner", None),
        P(None, "inner"),
        P(("outer", "inner"), None),
        P(),
    )
    return jax.shard_map(
        per_device,
        mesh=mesh,
        in_specs=placed,
        out_specs=P(("outer", "inner"), None),
        check_vma=False,
    )
```

profile of v0, /device:TPU:152, one launch (start us, length us, event | category | flops | bytes accessed | tf_op | source)
XLA Modules:
  0.0 284.8 jit_solution(12477237379816694622)
XLA Ops:
  6.5 0.7 all-gather.3.cloned.1.call-update
  7.3 0.7 all-gather.5.cloned.1.call-update
  8.0 0.7 maximum_bitcast_fusion
  8.7 0.7 compare_bitcast_fusion
  9.6 0.4 fusion.2
  10.3 139.8 %all-gather.3.cloned.1.call-done = bf16[2048,3072]{1,0:T(8,128)(2,1)} async-done(((bf16[128,3072]{1,0:T(8,128)(2,1)}), bf16[2048,3072]{1,0:T(8,128)(2,1)}) %all-gather.3.cloned.1.call-update) | async-done | bytes 12582928 | tf_op jit(solution)/shard_map/all_gather | solution.py:36
  150.1 8.2 %convolution_convert_fusion = bf16[256,3072]{1,0:T(8,128)(2,1)S(1)} fusion(bf16[2048,3072]{1,0:T(8,128)(2,1)} %all-gather.3.cloned.1.call-done, bf16[256,2048]{1,0:T(8,128)(2,1)S(1)} %copy-done, f32[256]{0:T(256)S(1)} %add_rsqrt_fusion, f32[256]{0:T(256)S(1)} %broadcast_multiply_fusion), kind=kOutput, calls=%fused_computation | convolution fusion | flops 3224109056 | bytes 15206400 | tf_op jit(solution)/shard_map/dot_general | solution.py:34
  158.5 1.9 collective-permute-start
  160.4 9.7 %collective-permute-start.1 = (bf16[1,256,2048]{2,1,0:T(8,128)(2,1)S(1)}, bf16[1,256,2048]{2,1,0:T(8,128)(2,1)S(1)}, u32[]{:S(2)}, u32[]{:S(2)}) collective-permute-start(bf16[1,256,2048]{2,1,0:T(8,128)(2,1)S(1)} %slice_bitcast_fusion), channel_id=1, source_target_pairs={{16,0},{32,16},{48,32},{64,48},{80,64},{96,80},{112,96},{128,112},... | collective-permute-start | bytes 3145736 | tf_op jit(solution)/shard_map/ppermute | solution.py:17
  170.1 5.2 %collective-permute-start.2 = (bf16[1,256,2048]{2,1,0:T(8,128)(2,1)S(1)}, bf16[1,256,2048]{2,1,0:T(8,128)(2,1)S(1)}, u32[]{:S(2)}, u32[]{:S(2)}) collective-permute-start(bf16[1,256,2048]{2,1,0:T(8,128)(2,1)S(1)} %slice_bitcast_fusion), channel_id=1, source_target_pairs={{0,1},{1,2},{2,3},{3,4},{4,5},{5,6},{6,7},{7,8},{8,9},{9,10},{10,1... | collective-permute-start | bytes 3145736 | tf_op jit(solution)/shard_map/ppermute | solution.py:14
  175.3 2.1 collective-permute-start.3
  178.8 20.7 %collective-permute-done = bf16[1,256,2048]{2,1,0:T(8,128)(2,1)S(1)} collective-permute-done((bf16[1,256,2048]{2,1,0:T(8,128)(2,1)S(1)}, bf16[1,256,2048]{2,1,0:T(8,128)(2,1)S(1)}, u32[]{:S(2)}, u32[]{:S(2)}) %collective-permute-start) | collective-permute-done | bytes 1048608 | tf_op jit(solution)/shard_map/ppermute | solution.py:14
  199.9 6.6 %collective-permute-done.1 = bf16[1,256,2048]{2,1,0:T(8,128)(2,1)S(1)} collective-permute-done((bf16[1,256,2048]{2,1,0:T(8,128)(2,1)S(1)}, bf16[1,256,2048]{2,1,0:T(8,128)(2,1)S(1)}, u32[]{:S(2)}, u32[]{:S(2)}) %collective-permute-start.1) | collective-permute-done | bytes 1048608 | tf_op jit(solution)/shard_map/ppermute | solution.py:17
  206.9 21.2 %collective-permute-done.2 = bf16[1,256,2048]{2,1,0:T(8,128)(2,1)S(1)} collective-permute-done((bf16[1,256,2048]{2,1,0:T(8,128)(2,1)S(1)}, bf16[1,256,2048]{2,1,0:T(8,128)(2,1)S(1)}, u32[]{:S(2)}, u32[]{:S(2)}) %collective-permute-start.2) | collective-permute-done | bytes 1048608 | tf_op jit(solution)/shard_map/ppermute | solution.py:14
  228.4 26.1 %collective-permute-done.3 = bf16[1,256,2048]{2,1,0:T(8,128)(2,1)S(1)} collective-permute-done((bf16[1,256,2048]{2,1,0:T(8,128)(2,1)S(1)}, bf16[1,256,2048]{2,1,0:T(8,128)(2,1)S(1)}, u32[]{:S(2)}, u32[]{:S(2)}) %collective-permute-start.3) | collective-permute-done | bytes 1048608 | tf_op jit(solution)/shard_map/ppermute | solution.py:17
  259.6 0.4 fusion.11
  259.9 2.0 fusion.69
  262.6 2.3 fusion.67
  271.8 0.2 fusion.49
  272.3 0.2 fusion.45
  272.5 0.2 fusion.43
  272.8 0.2 fusion.41
  273.1 0.2 fusion.39
  273.6 4.4 %convolution_convert_fusion.1 = bf16[256,2048]{1,0:T(8,128)(2,1)} fusion(bf16[256,1024]{1,0:T(8,128)(2,1)S(1)} %fusion.37, bf16[1024,2048]{1,0:T(8,128)(2,1)} %all-gather.5.cloned.1.call-done), kind=kOutput, calls=%fused_computation.3 | convolution fusion | flops 1074266112 | bytes 5767168 | tf_op jit(solution)/shard_map/dot_general | solution.py:86
  (89 shorter events, 15.9 us)
Async XLA Ops:
  6.5 2.8 copy-start
  6.5 143.5 %all-gather.3.cloned.1.call-start = ((), (), s32[]{:S(2)}) async-start(), calls=%async_computation | async-start | bytes 13369344 | tf_op jit(solution)/shard_map/all_gather | solution.py:36
  7.3 2.7 copy-start.1
  7.3 266.3 %all-gather.5.cloned.1.call-start = ((), (), s32[]{:S(2)}) async-start(), calls=%async_computation.1 | async-start | bytes 4456448 | tf_op jit(solution)/shard_map/all_gather | solution.py:88
  158.5 41.0 %collective-permute-start = (bf16[1,256,2048]{2,1,0:T(8,128)(2,1)S(1)}, bf16[1,256,2048]{2,1,0:T(8,128)(2,1)S(1)}, u32[]{:S(2)}, u32[]{:S(2)}) collective-permute-start(bf16[1,256,2048]{2,1,0:T(8,128)(2,1)S(1)} %slice_bitcast_fusion), channel_id=1, source_target_pairs={{0,16},{16,32},{32,48},{48,64},{64,80},{80,96},{96,112},{112,128},... | collective-permute-start | bytes 3145736 | tf_op jit(solution)/shard_map/ppermute | solution.py:14
  160.4 46.0 %collective-permute-start.1 = (bf16[1,256,2048]{2,1,0:T(8,128)(2,1)S(1)}, bf16[1,256,2048]{2,1,0:T(8,128)(2,1)S(1)}, u32[]{:S(2)}, u32[]{:S(2)}) collective-permute-start(bf16[1,256,2048]{2,1,0:T(8,128)(2,1)S(1)} %slice_bitcast_fusion), channel_id=1, source_target_pairs={{16,0},{32,16},{48,32},{64,48},{80,64},{96,80},{112,96},{128,112},... | collective-permute-start | bytes 3145736 | tf_op jit(solution)/shard_map/ppermute | solution.py:17
  170.1 57.9 %collective-permute-start.2 = (bf16[1,256,2048]{2,1,0:T(8,128)(2,1)S(1)}, bf16[1,256,2048]{2,1,0:T(8,128)(2,1)S(1)}, u32[]{:S(2)}, u32[]{:S(2)}) collective-permute-start(bf16[1,256,2048]{2,1,0:T(8,128)(2,1)S(1)} %slice_bitcast_fusion), channel_id=1, source_target_pairs={{0,1},{1,2},{2,3},{3,4},{4,5},{5,6},{6,7},{7,8},{8,9},{9,10},{10,1... | collective-permute-start | bytes 3145736 | tf_op jit(solution)/shard_map/ppermute | solution.py:14
  175.3 79.2 %collective-permute-start.3 = (bf16[1,256,2048]{2,1,0:T(8,128)(2,1)S(1)}, bf16[1,256,2048]{2,1,0:T(8,128)(2,1)S(1)}, u32[]{:S(2)}, u32[]{:S(2)}) collective-permute-start(bf16[1,256,2048]{2,1,0:T(8,128)(2,1)S(1)} %slice_bitcast_fusion), channel_id=1, source_target_pairs={{1,0},{2,1},{3,2},{4,3},{5,4},{6,5},{7,6},{8,7},{9,8},{10,9},{11,1... | collective-permute-start | bytes 3145736 | tf_op jit(solution)/shard_map/ppermute | solution.py:17
Sparse Core Ops, SparseCore 0:
  9.1 140.9 all-gather.2
  151.8 107.4 all-gather.4
where the time goes:
time: 285 us
  waiting for transfers between devices  216 us (76%)
  matrix products  29 us (10%)
  starting transfers between devices  18.9 us (7%)
  between operations  14.1 us (5%)
  other arithmetic  6.84 us (2%)
    all_gather x1, waiting for transfers between devices, per_device(): lax.all_gather(w_qkv, 'inner', axis=0, tiled=True)  140 us
    ppermute x2, waiting for transfers between devices, padded(): lax.ppermute(lax.slice_in_dim(block, block.shape[dim] - width, None, axis...  41.9 us
    ppermute x2, waiting for transfers between devices, padded(): lax.ppermute(lax.slice_in_dim(block, 0, width, axis=dim), axis, backward)  32.8 us
    ppermute x2, starting transfers between devices, padded(): lax.ppermute(lax.slice_in_dim(block, 0, width, axis=dim), axis, backward)  11.8 us
    dot_general x40, matrix products, per_device(): jnp.dot(rounded[:, slot_no * rows_here:(slot_no + 1) * rows_here], candid...  9.07 us
    dot_general x1, matrix products, per_device(): jnp.dot(normed, lax.all_gather(w_qkv, 'inner', axis=0, tiled=True), prefe...  8.16 us
    dot_general x40, matrix products, per_device(): jnp.einsum('qd,kd->qk', query_head, source_kv[:, offset_q:offset_q + head...  7.37 us
    ppermute x2, starting transfers between devices, padded(): lax.ppermute(lax.slice_in_dim(block, block.shape[dim] - width, None, axis...  7.12 us
  transfers between devices with their start and end apart: 6, of which 5 were waited for; matrix products, arithmetic and copies ran while one was open for 11% of the time, Pallas kernels for 0%

commit v1 on v0

v1 whole, which is shorter than its diff:
```python
import functools
import math

import jax
import jax.numpy as jnp
from jax import lax
from jax.experimental import pallas as pl
from jax.experimental.pallas import tpu as pltpu
from jax.sharding import PartitionSpec as P

MESH = pl.DeviceIdType.MESH
HD = 128
EXP_SCALE = float(HD) ** (-0.5) * math.log2(math.e)
K, V, Q, O = 0, 1, 2, 3
SPLIT_X = {K: False, V: True, Q: True, O: False}
Z_FIRST = {K: True, V: True, Q: True, O: False}


def kernel(tokens, w_qkv, w_out, listed, counts, out, w, kv, queries, context, normed, tok, relay_buf,
           load_sem, tok_sem, recv_ring, send_ring, recv_mate, send_mate, recv_halo, send_halo, recv_relay, send_relay):
    o, i = lax.axis_index("outer"), lax.axis_index("inner")
    div, rem = lax.div, lax.rem
    x, c = rem(div(o, 2), 4), rem(o, 2)
    zl, y = div(i, 4), rem(i, 4)
    z = div(o, 8) * 4 + zl

    def dev(x, y, z, c):
        x, y, z = rem(x + 4, 4), rem(y + 4, 4), rem(z + 8, 8)
        return (div(z, 4) * 8 + x * 2 + c, rem(z, 4) * 4 + y)

    sign = 1 - 2 * c
    mate = dev(x, y, z, 1 - c)
    half = 4 * c
    outward_sign = 2 * c - 1
    outward = dev(x + outward_sign, y, z, 1 - c)
    is_edge = ((c == 0) & (x == 0)) | ((c == 1) & (x == 3))
    is_source = ((c == 0) & (z >= 4)) | ((c == 1) & (z < 4))
    edge_source = is_edge & is_source
    edge_end = is_edge & jnp.logical_not(is_source)
    inside = jnp.logical_not(is_edge)
    across_up = (y == 3) & (zl < 3)
    across_down = (y == 0) & (zl > 0)
    middle = (z >= 2) & (z <= 5)
    relay_sign = jnp.where(middle, 1, -1) * jnp.where(c == 0, 1, -1)
    relay_half = jnp.where(relay_sign > 0, 0, 1)

    loads = []

    def load_block(p, h, n):
        if p == O:
            src = w_out.at[pl.ds(pl.multiple_of(128 * h, 128), 128), :]
        else:
            base = {Q: 0, K: 1024, V: 2048}[p]
            src = w_qkv.at[:, pl.ds(pl.multiple_of(base + 128 * h, 128), 128)]
        copy = pltpu.make_async_copy(src, w.at[p, h, zl, y], load_sem.at[n])
        copy.start()
        return copy

    own_loads = {}
    number = 0
    for p in (V, K, Q, O):
        if SPLIT_X[p]:
            own_loads[p] = [load_block(p, half + x, number)]
            number += 1
        else:
            own_loads[p] = [load_block(p, half + j, number + j) for j in range(4)]
            number += 4
    tok_copy = pltpu.make_async_copy(tokens, tok, tok_sem)
    tok_copy.start()

    barrier = pltpu.get_barrier_semaphore()

    def greet(device):
        pl.semaphore_signal(barrier, inc=1, device_id=device, device_id_type=MESH)

    for device in (dev(x, y, z + 1, c), dev(x, y, z - 1, c), dev(x, y + 1, z, c), dev(x, y - 1, z, c),
                   dev(x + 1, y, z, c), dev(x - 1, y, z, c), mate):
        greet(device)

    @pl.when(inside)
    def _():
        greet(outward)

    @pl.when(is_edge)
    def _():
        for step in (2, -2):
            greet(dev(x + outward_sign, y, z + step, 1 - c))
            greet(dev(x, y, z + step, c))

    @pl.when(across_up)
    def _():
        greet(dev(x, 0, z + 1, c))

    @pl.when(across_down)
    def _():
        greet(dev(x, 3, z - 1, c))

    count = lambda pred: jnp.where(pred, 1, 0)
    pl.semaphore_wait(barrier, 8 + 3 * count(is_edge) + count(across_up) + count(across_down))

    sends = []

    def remote(src, dst, send, recv, device):
        return pltpu.make_async_remote_copy(
            src_ref=src, dst_ref=dst, send_sem=send, recv_sem=recv, device_id=device, device_id_type=MESH)

    def arrived(ref, recv):
        remote(ref, ref, send_mate.at[0, 0], recv, mate).wait_recv()

    def along(axis, step):
        return {"z": dev(x, y, z + step, c), "y": dev(x, y + step, z, c), "x": dev(x + step, y, z, c)}[axis]

    here = {"z": zl, "y": y, "x": x}

    def at(axis, step):
        return rem(here[axis] + step + 4, 4)

    def heads_of(p):
        return half + x if SPLIT_X[p] else pl.ds(half, 4)

    def first_axis(p):
        return "z" if Z_FIRST[p] else "y"

    def second_axis(p):
        return "y" if Z_FIRST[p] else "z"

    def ref_first(p, step):
        hs = heads_of(p)
        return w.at[p, hs, at("z", step), y] if Z_FIRST[p] else w.at[p, hs, zl, at("y", step)]

    def ref_second(p, step):
        hs = heads_of(p)
        return w.at[p, hs, :, at("y", step)] if Z_FIRST[p] else w.at[p, hs, at("z", step)]

    def ref_x(p, step):
        return w.at[p, half + at("x", step)]

    STAGES = {0: (ref_first, first_axis), 1: (ref_second, second_axis), 2: (ref_x, lambda p: "x")}

    def ring_send(p, stage, ref, slot, step):
        axis = STAGES[stage][1](p)
        copy = remote(ref, ref, send_ring.at[p, stage, slot], recv_ring.at[p, stage, slot], along(axis, step))
        copy.start()
        sends.append(copy)

    def ring_start(p, stage):
        ref = STAGES[stage][0](p, 0)
        ring_send(p, stage, ref, 0, 1)
        ring_send(p, stage, ref, 1, -1)

    def ring_relay(p, stage):
        ref = STAGES[stage][0](p, -sign)
        arrived(ref, recv_ring.at[p, stage, c])
        ring_send(p, stage, ref, 2, sign)
        return ref

    def ring_finish(p, stage):
        ref = STAGES[stage][0]
        a, b = ref(p, sign), ref(p, 2)
        arrived(a, recv_ring.at[p, stage, 1 - c])
        arrived(b, recv_ring.at[p, stage, 2])
        return a, b

    def to_mate(p, n, ref):
        copy = remote(ref, ref, send_mate.at[p, n], recv_mate.at[p, n], mate)
        copy.start()
        sends.append(copy)

    other = 4 * (1 - c)

    def from_mate(p):
        for n in range(4):
            if SPLIT_X[p]:
                step = {0: 0, 1: sign, 2: -sign, 3: 2}[n]
                ref = w.at[p, other + rem(x + step + 4, 4)]
            else:
                step = {0: 0, 1: sign, 2: -sign, 3: 2}[n]
                axis = second_axis(p)
                ref = (w.at[p, pl.ds(other, 4), :, at("y", step)] if axis == "y"
                       else w.at[p, pl.ds(other, 4), at("z", step)])
            arrived(ref, recv_mate.at[p, n])

    def first_start(p):
        for copy in own_loads[p]:
            copy.wait()
        ring_start(p, 0)

    def first_relay(p):
        ring_relay(p, 0)

    def second_start(p):
        ring_finish(p, 0)
        ring_start(p, 1)
        if not SPLIT_X[p]:
            to_mate(p, 0, ref_second(p, 0))

    def second_relay(p):
        ref = ring_relay(p, 1)
        if not SPLIT_X[p]:
            to_mate(p, 1, ref)

    def second_finish(p):
        a, b = ring_finish(p, 1)
        if SPLIT_X[p]:
            ring_start(p, 2)
            to_mate(p, 0, ref_x(p, 0))
        else:
            to_mate(p, 2, a)
            to_mate(p, 3, b)

    def x_relay(p):
        to_mate(p, 1, ring_relay(p, 2))

    def x_finish(p):
        a, b = ring_finish(p, 2)
        to_mate(p, 2, a)
        to_mate(p, 3, b)

    def normalize():
        tok_copy.wait()

        def body(n, _):
            rows = pl.ds(pl.multiple_of(n * 32, 32), 32)
            values = tok[rows, :].astype(jnp.float32)
            center = values - jnp.mean(values, axis=-1, keepdims=True)
            spread = jnp.mean(center * center, axis=-1, keepdims=True)
            normed[rows, :] = (center * lax.rsqrt(spread + 1e-05)).astype(jnp.bfloat16)
            return 0

        lax.fori_loop(0, 8, body, 0)

    def pair_of(p, h):
        return jnp.concatenate([w[p, h].reshape(2048, 128), w[p, h + 1].reshape(2048, 128)], axis=1)

    def project(p, first):
        def body(j, _):
            h = first + 2 * j
            result = jnp.dot(normed[...], pair_of(p, h), preferred_element_type=jnp.float32).astype(jnp.bfloat16)
            for k in range(2):
                part = result[:, 128 * k:128 * (k + 1)]
                if p == Q:
                    queries[h + k] = part
                else:
                    kv[0, h + k, p] = part
            return 0

        lax.fori_loop(0, 2, body, 0)

    def group(slot, g):
        return kv.at[slot, pl.ds(2 * g, 2)]

    cond_sends = []

    def when_send(pred, copy):
        @pl.when(pred)
        def _():
            copy.start()
        cond_sends.append((pred, copy))

    def local(slot, g):
        return pltpu.make_async_copy(group(0, g), group(slot, g), recv_halo.at[slot - 1, g])

    def halo_send(g):
        src = group(0, g)
        copy = remote(src, group(1 + c, g), send_halo.at[0, g], recv_halo.at[c, g], mate)
        copy.start()
        sends.append(copy)
        when_send(inside, remote(src, group(2 - c, g), send_halo.at[1, g], recv_halo.at[1 - c, g], outward))
        step = 2 if g % 2 == 0 else -2
        when_send(edge_source, remote(src, relay_buf.at[g // 2], send_halo.at[1, g], recv_relay.at[g // 2],
                                      dev(x + outward_sign, y, z + step, 1 - c)))

        @pl.when(edge_end)
        def _():
            local(1 + c, g).start()

        up, down = (o, jnp.minimum(i + 1, 15)), (o, jnp.maximum(i - 1, 0))
        when_send(i < 15, remote(src, group(3, g), send_halo.at[2, g], recv_halo.at[2, g], up))
        when_send(i > 0, remote(src, group(4, g), send_halo.at[3, g], recv_halo.at[3, g], down))

        @pl.when(i == 15)
        def _():
            local(4, g).start()

        @pl.when(i == 0)
        def _():
            local(3, g).start()

    def halo_relay():
        @pl.when(is_edge)
        def _():
            for k in range(2):
                arrived(relay_buf.at[k], recv_relay.at[k])
                g = 2 * k + relay_half
                remote(relay_buf.at[k], group(1 + c, g), send_relay.at[k], recv_halo.at[c, g],
                       dev(x, y, z + 2 * relay_sign, c)).start()

    def halo_relay_end():
        @pl.when(is_edge)
        def _():
            for k in range(2):
                g = 2 * k + relay_half
                remote(relay_buf.at[k], group(1 + c, g), send_relay.at[k], recv_halo.at[c, g],
                       dev(x, y, z + 2 * relay_sign, c)).wait_send()

    ids = lax.broadcasted_iota(jnp.int32, (1, 256), 1)
    masks = []
    for n in range(5):
        one = listed[0:1, n:n + 1]
        length = jnp.sum(jnp.where(ids == jnp.maximum(one, 0), counts[...], 0), axis=1, keepdims=True)
        masks.append(jnp.where((one >= 0) & (ids < length), 0.0, -jnp.inf).astype(jnp.float32))

    def attend(h):
        query = queries[h]
        scores = []
        for n in range(5):
            s = lax.dot_general(query, kv[n, h, 0], (((1,), (1,)), ((), ())), preferred_element_type=jnp.float32)
            scores.append(s + masks[n])
        top = scores[0]
        for n in range(1, 5):
            top = jnp.maximum(top, scores[n])
        largest = jnp.max(top, axis=1, keepdims=True)
        total = None
        acc = None
        for n in range(5):
            weight = jnp.exp2((scores[n] - largest) * EXP_SCALE)
            total = weight if total is None else total + weight
            part = jnp.dot(weight.astype(jnp.bfloat16), kv[n, h, 1], preferred_element_type=jnp.float32)
            acc = part if acc is None else acc + part
        totals = jnp.sum(total, axis=1, keepdims=True)
        context[:, pl.ds(pl.multiple_of(128 * h, 128), 128)] = (acc / totals).astype(jnp.bfloat16)

    def attention_group(g, _):
        for slot in range(1, 5):
            arrived(kv.at[slot, pl.ds(2 * g, 2)], recv_halo.at[slot - 1, g])

        def body(k, _):
            attend(2 * g + k)
            return 0

        lax.fori_loop(0, 2, body, 0)
        return 0

    def out_project():
        def body(n, _):
            zz, yy = div(n, 2), 2 * rem(n, 2)
            weights = jnp.concatenate(
                [w[O, :, zz, yy].reshape(1024, 128), w[O, :, zz, yy + 1].reshape(1024, 128)], axis=1)
            result = jnp.dot(context[...], weights, preferred_element_type=jnp.float32)
            out[:, pl.ds(pl.multiple_of(n * 256, 256), 256)] = result.astype(jnp.bfloat16)
            return 0

        lax.fori_loop(0, 8, body, 0)

    for p in (V, K, Q, O):
        first_start(p)
    first_relay(V)
    first_relay(K)
    second_start(V)
    second_start(K)
    first_relay(Q)
    first_relay(O)
    normalize()
    second_relay(V)
    second_finish(V)
    second_start(Q)
    second_start(O)
    second_relay(K)
    x_relay(V)
    second_relay(Q)
    second_finish(K)
    second_finish(Q)
    project(K, half)
    x_finish(V)
    project(V, half)
    from_mate(K)
    project(K, other)
    from_mate(V)
    project(V, other)
    for g in range(4):
        halo_send(g)
    second_relay(O)
    x_relay(Q)
    second_finish(O)
    x_finish(Q)
    project(Q, half)
    from_mate(Q)
    project(Q, other)
    halo_relay()
    lax.fori_loop(0, 4, attention_group, 0)
    from_mate(O)
    out_project()
    for copy in sends:
        copy.wait_send()
    for pred, copy in cond_sends:
        @pl.when(pred)
        def _(copy=copy):
            copy.wait_send()
    halo_relay_end()


def per_device(tokens, w_qkv, w_out, neighbours, counts):
    dma = pltpu.SemaphoreType.DMA
    vmem, hbm = pl.BlockSpec(memory_space=pltpu.VMEM), pl.BlockSpec(memory_space=pl.ANY)
    bf16 = jnp.bfloat16
    return pl.pallas_call(
        kernel,
        out_shape=jax.ShapeDtypeStruct((256, 2048), bf16),
        in_specs=[hbm, hbm, hbm, vmem, vmem],
        out_specs=vmem,
        scratch_shapes=[
            pltpu.VMEM((4, 8, 4, 4, 128, 128), bf16),
            pltpu.VMEM((5, 8, 2, 256, 128), bf16),
            pltpu.VMEM((8, 256, 128), bf16),
            pltpu.VMEM((256, 1024), bf16),
            pltpu.VMEM((256, 2048), bf16),
            pltpu.VMEM((256, 2048), bf16),
            pltpu.VMEM((2, 2, 2, 256, 128), bf16),
            dma((10,)), dma,
            dma((4, 3, 3)), dma((4, 3, 3)),
            dma((4, 4)), dma((4, 4)),
            dma((4, 4)), dma((4, 4)),
            dma((2,)), dma((2,)),
        ],
        compiler_params=pltpu.CompilerParams(
            collective_id=0, has_side_effects=True, vmem_limit_bytes=60 << 20),
    )(tokens, w_qkv, w_out, neighbours, counts.reshape(1, 256))


def solution(mesh):
    placed = (P(("outer", "inner"), None), P("inner", None), P(None, "inner"), P(("outer", "inner"), None), P())
    return jax.shard_map(
        per_device, mesh=mesh, in_specs=placed, out_specs=P(("outer", "inner"), None), check_vma=False)
```

time: 285 us -> 128 us (0.45)
  waiting for transfers between devices: 216 us -> 0 us
  Pallas kernels: 0 us -> 125 us
  matrix products: 29 us -> 0 us
  starting transfers between devices: 18.9 us -> 0 us
  between operations: 14.1 us -> 0.01 us
  other arithmetic: 6.84 us -> 0 us
    all_gather x2 -> x0, waiting for transfers between devices: 140 us -> none  [the longest x1 140 us: per_device(): lax.all_gather(w_qkv, 'inner', axis=0, tiled=True)]
    pallas_call x0 -> x1, Pallas kernels: none -> 125 us  [per_device(): pl.pallas_call(kernel, out_shape=jax.ShapeDtypeStruct((256, 2048), bf16),...]
    ppermute x4 -> x0, waiting for transfers between devices: 74.6 us -> none  [the longest x2 41.9 us: padded(): lax.ppermute(lax.slice_in_dim(block, block.shape[dim] - width, None, axis...]
    dot_general x82 -> x0, matrix products: 29 us -> none  [the longest x40 9.07 us: per_device(): jnp.dot(rounded[:, slot_no * rows_here:(slot_no + 1) * rows_here], candid...]
    ppermute x4 -> x0, starting transfers between devices: 18.9 us -> none  [the longest x2 11.8 us: padded(): lax.ppermute(lax.slice_in_dim(block, 0, width, axis=dim), axis, backward)]
    reduce_sum x5 -> x0, other arithmetic: 5.08 us -> none  [the longest x2 4.26 us: per_device(): totals = jnp.sum(weights, axis=1, keepdims=True)]
  transfers between devices with their start and end apart: 6 -> 0, of which waited for: 5 -> 0; matrix products, arithmetic and copies ran while one was open for 11% -> 0% of each run, Pallas kernels for 0% -> 0%
where the time goes in v1:
time: 128 us; the launch traced here: 127 us
  Pallas kernels  125 us (98%)
  local copies, waits for them, and re-layouts  2.3 us (2%)
    pallas_call x1, Pallas kernels, per_device(): pl.pallas_call(kernel, out_shape=jax.ShapeDtypeStruct((256, 2048), bf16),...  125 us

profile of v1, /device:TPU:152, one launch (start us, length us, event | category | flops | bytes accessed | tf_op | source)
XLA Modules:
  0.0 127.4 jit_solution(6216779173134113808)
XLA Ops:
  0.0 125.1 %shard_map.55 = bf16[256,2048]{1,0:T(8,128)(2,1)} custom-call(bf16[256,2048]{1,0:T(8,128)(2,1)} %tokens.1, bf16[128,3072]{1,0:T(8,128)(2,1)} %w_qkv.1, bf16[1024,128]{1,0:T(8,128)(2,1)} %w_out.1, s32[1,5]{1,0:T(1,128)} %listed.1, s32[1,256]{1,0:T(1,128)} %bitcast.1), custom_call_target="tpu_custom_call" | custom-call | tf_op jit(solution)/shard_map/pallas_call | solution.py:406
  125.1 2.3 %copy.7 = bf16[256,2048]{1,0:T(8,128)(2,1)} copy(bf16[256,2048]{1,0:T(8,128)(2,1)} %shard_map.55) | data formatting | bytes 2097152

commit v2 on v0

v2 whole, which is shorter than its diff:
```python
import math

import jax
import jax.numpy as jnp
from jax import lax
from jax.experimental import pallas as pl
from jax.experimental.pallas import tpu as pltpu
from jax.sharding import PartitionSpec as P

MESH = pl.DeviceIdType.MESH
HD = 128
EXP_SCALE = float(HD) ** (-0.5) * math.log2(math.e)
Q, K, V, O0, O1 = 0, 1, 2, 3, 4
Z_FIRST = {Q: True, K: True, V: False, O0: True, O1: False}
CHUNKS = 2
ROWS = 256 // CHUNKS


def kernel(tokens, w_qkv, w_out, listed, counts, out, wh, wo, raw, normed, queries, kv, above, below, masks, ctx_out, ctx,
           load_sem, tok_sem, recv_ring, send_ring, recv_mate, send_mate, recv_tok, send_tok, recv_tmate, send_tmate,
           recv_mask, send_mask, recv_up, recv_down, send_up, send_down, recv_edge, send_edge, recv_ctx, send_ctx):
    o, i = lax.axis_index("outer"), lax.axis_index("inner")
    div, rem = lax.div, lax.rem
    x, c = rem(div(o, 2), 4), rem(o, 2)
    zl, y = div(i, 4), rem(i, 4)
    zh = div(o, 8)
    z = zh * 4 + zl
    me = 2 * x + c

    def dev(x, y, z, c):
        x, y, z = rem(x + 4, 4), rem(y + 4, 4), rem(z + 8, 8)
        return (div(z, 4) * 8 + x * 2 + c, rem(z, 4) * 4 + y)

    def owner(j):
        return (zh * 8 + j, i)

    sign = 1 - 2 * c
    mate = dev(x, y, z, 1 - c)
    half, other = 4 * c, 4 * (1 - c)
    across_up = (y == 3) & (zl < 3)
    across_down = (y == 0) & (zl > 0)

    tok_copy = pltpu.make_async_copy(tokens, raw, tok_sem)
    tok_copy.start()
    own_loads = {}
    for p in (K, V, Q):
        src = w_qkv.at[:, pl.ds(pl.multiple_of(1024 * p + 128 * me, 128), 128)]
        own_loads[p] = [pltpu.make_async_copy(src, wh.at[p, zl, y], load_sem.at[p])]
    for p in (O0, O1):
        own_loads[p] = []
        for k in range(2):
            r = half + 2 * (p - O0) + k
            src = w_out.at[pl.ds(pl.multiple_of(128 * r, 128), 128), :]
            own_loads[p].append(pltpu.make_async_copy(src, wo.at[r, zl, y], load_sem.at[3 + 2 * (p - O0) + k]))
    for copies in own_loads.values():
        for copy in copies:
            copy.start()

    barrier = pltpu.get_barrier_semaphore()

    def greet(device):
        pl.semaphore_signal(barrier, inc=1, device_id=device, device_id_type=MESH)

    peers = [owner(rem(me + k, 8)) for k in range(1, 8)]
    peers += [dev(x, y, z + 1, c), dev(x, y, z - 1, c), dev(x, y + 1, z, c), dev(x, y - 1, z, c),
              dev(x, y, z + 2, c), dev(x, y, z - 2, c), dev(x, y + 2, z, c), dev(x, y, z + 4, c)]
    for device in peers:
        greet(device)

    @pl.when(across_up)
    def _():
        greet(dev(x, 0, z + 1, c))

    @pl.when(across_down)
    def _():
        greet(dev(x, 3, z - 1, c))

    tok_copy.wait()

    def normalize(n, _):
        rows = pl.ds(pl.multiple_of(n * 32, 32), 32)
        values = raw[rows, :].astype(jnp.float32)
        center = values - jnp.mean(values, axis=-1, keepdims=True)
        spread = jnp.mean(center * center, axis=-1, keepdims=True)
        normed[me, rows, :] = (center * lax.rsqrt(spread + 1e-05)).astype(jnp.bfloat16)
        return 0

    lax.fori_loop(0, 8, normalize, 0)

    ids = lax.broadcasted_iota(jnp.int32, (1, 256), 1)
    for n in range(5):
        one = listed[0:1, n:n + 1]
        length = jnp.sum(jnp.where(ids == jnp.maximum(one, 0), counts[...], 0), axis=1, keepdims=True)
        masks[me, n:n + 1, :] = jnp.where((one >= 0) & (ids < length), 0.0, -jnp.inf).astype(jnp.float32)

    zero = jnp.zeros((2, 256, 128), jnp.bfloat16)
    kv[9 * zh] = zero

    @pl.when(i == 15)
    def _():
        def fill(n, _):
            above[n] = zero
            return 0
        lax.fori_loop(0, 8, fill, 0)

    @pl.when(i == 0)
    def _():
        def fill(n, _):
            below[n] = zero
            return 0
        lax.fori_loop(0, 8, fill, 0)

    def count(pred):
        return jnp.where(pred, 1, 0)

    pl.semaphore_wait(barrier, len(peers) + count(across_up) + count(across_down))

    sends = []

    def remote(src, dst, send, recv, device):
        return pltpu.make_async_remote_copy(
            src_ref=src, dst_ref=dst, send_sem=send, recv_sem=recv, device_id=device, device_id_type=MESH)

    def go(src, dst, send, recv, device):
        copy = remote(src, dst, send, recv, device)
        copy.start()
        sends.append(copy)

    def arrived(ref, recv):
        remote(ref, ref, send_mate.at[0, 0], recv, mate).wait_recv()

    here = {"z": zl, "y": y}

    def at(axis, step):
        return rem(here[axis] + step + 4, 4)

    def along(axis, step):
        return dev(x, y, z + step, c) if axis == "z" else dev(x, y + step, z, c)

    def piece(p):
        if p < O0:
            return wh.at[p]
        return wo.at[pl.ds(half + 2 * (p - O0), 2)]

    def block(p, zi, yi):
        return wh.at[p, zi, yi] if p < O0 else wo.at[pl.ds(half + 2 * (p - O0), 2), zi, yi]

    def axis_of(p, stage):
        return "z" if Z_FIRST[p] == (stage == 0) else "y"

    def part(p, stage, step):
        if stage == 0:
            return block(p, at("z", step), y) if Z_FIRST[p] else block(p, zl, at("y", step))
        return block(p, slice(None), at("y", step)) if Z_FIRST[p] else block(p, at("z", step), slice(None))

    def ring_send(p, stage, ref, slot, step):
        go(ref, ref, send_ring.at[p, stage, slot], recv_ring.at[p, stage, slot], along(axis_of(p, stage), step))

    def ring_start(p, stage, direct=False):
        ref = part(p, stage, 0)
        ring_send(p, stage, ref, 0, 1)
        ring_send(p, stage, ref, 1, -1)
        if direct:
            ring_send(p, stage, ref, 2, 2 * sign)

    def ring_relay(p, stage):
        ref = part(p, stage, -sign)
        arrived(ref, recv_ring.at[p, stage, c])
        ring_send(p, stage, ref, 2, sign)
        return ref

    def ring_finish(p, stage, direct=False):
        if direct:
            arrived(part(p, stage, -sign), recv_ring.at[p, stage, c])
        a, b = part(p, stage, sign), part(p, stage, 2)
        arrived(a, recv_ring.at[p, stage, 1 - c])
        arrived(b, recv_ring.at[p, stage, 2])
        return a, b

    def to_mate(p, n, ref):
        go(ref, ref, send_mate.at[p - O0, n], recv_mate.at[p - O0, n], mate)

    def from_mate(p):
        rows = pl.ds(other + 2 * (p - O0), 2)
        for n, step in ((0, 0), (1, sign), (2, -sign), (3, 2)):
            ref = (wo.at[rows, :, at("y", step)] if Z_FIRST[p] else wo.at[rows, at("z", step)])
            arrived(ref, recv_mate.at[p - O0, n])

    def first_start(p):
        for copy in own_loads[p]:
            copy.wait()
        ring_start(p, 0, p < O0)

    def second_start(p):
        ring_finish(p, 0, p < O0)
        ring_start(p, 1, p < O0)
        if p >= O0:
            to_mate(p, 0, part(p, 1, 0))

    def second_relay(p):
        to_mate(p, 1, ring_relay(p, 1))

    def second_finish(p):
        a, b = ring_finish(p, 1)
        to_mate(p, 2, a)
        to_mate(p, 3, b)

    def rows_of(j, n):
        return normed.at[j, pl.ds(n * ROWS, ROWS)]

    def slab(step, core):
        return 2 * rem(x + step + 4, 4) + core

    def tok_start():
        for n in range(CHUNKS):
            ref = rows_of(me, n)
            go(ref, ref, send_tok.at[0, n], recv_tok.at[0, n], dev(x + 1, y, z, c))
            go(ref, ref, send_tok.at[1, n], recv_tok.at[1, n], dev(x - 1, y, z, c))
            go(ref, ref, send_tmate.at[0, n], recv_tmate.at[0, n], mate)

    def tok_relay(n):
        ref = rows_of(slab(-sign, c), n)
        arrived(ref, recv_tok.at[c, n])
        go(ref, ref, send_tok.at[2, n], recv_tok.at[2, n], dev(x + sign, y, z, c))
        go(ref, ref, send_tmate.at[1, n], recv_tmate.at[1, n], mate)

    def tok_pass(n):
        ref = rows_of(slab(sign, c), n)
        arrived(ref, recv_tok.at[1 - c, n])
        go(ref, ref, send_tmate.at[2, n], recv_tmate.at[2, n], mate)

    def tok_last(n):
        ref = rows_of(slab(2, c), n)
        arrived(ref, recv_tok.at[2, n])
        go(ref, ref, send_tmate.at[3, n], recv_tmate.at[3, n], mate)

    def tok_mate(m):
        step = {0: 0, 1: sign, 2: -sign, 3: 2}[m]
        for n in range(CHUNKS):
            arrived(rows_of(slab(step, 1 - c), n), recv_tmate.at[m, n])

    conditional = []

    def when_go(pred, copy):
        @pl.when(pred)
        def _():
            copy.start()
        conditional.append((pred, copy))

    up, down = (o, jnp.minimum(i + 1, 15)), (o, jnp.maximum(i - 1, 0))
    edge_slab = 7 * (1 - zh)

    def project_kv(j):
        weights = jnp.concatenate([wh[K].reshape(2048, 128), wh[V].reshape(2048, 128)], axis=1)
        result = jnp.dot(normed[j], weights, preferred_element_type=jnp.float32).astype(jnp.bfloat16)
        kv[j + 1, 0] = result[:, :128]
        kv[j + 1, 1] = result[:, 128:]

    def halo_send(j):
        ref = kv.at[j + 1]
        when_go(i < 15, remote(ref, below.at[j], send_up.at[j], recv_down.at[j], up))
        when_go(i > 0, remote(ref, above.at[j], send_down.at[j], recv_up.at[j], down))
        when_go(j == edge_slab, remote(ref, kv.at[9 * zh], send_edge, recv_edge, dev(x, y, z + 4, c)))

    def project_q(j):
        queries[j] = jnp.dot(normed[j], wh[Q].reshape(2048, 128), preferred_element_type=jnp.float32).astype(jnp.bfloat16)

    def attend(j, target):
        @pl.when(i < 15)
        def _():
            arrived(above.at[j], recv_up.at[j])

        @pl.when(i > 0)
        def _():
            arrived(below.at[j], recv_down.at[j])

        @pl.when(j == edge_slab)
        def _():
            arrived(kv.at[9 * (1 - zh)], recv_edge)

        query = queries[j]
        pairs = (lambda n: kv[j + 1, n], lambda n: kv[j, n], lambda n: kv[j + 2, n], lambda n: below[j, n],
                 lambda n: above[j, n])
        scores = []
        for n in range(5):
            s = lax.dot_general(query, pairs[n](0), (((1,), (1,)), ((), ())), preferred_element_type=jnp.float32)
            scores.append(s + masks[j, n:n + 1, :])
        top = scores[0]
        for n in range(1, 5):
            top = jnp.maximum(top, scores[n])
        largest = jnp.max(top, axis=1, keepdims=True)
        total = None
        acc = None
        for n in range(5):
            weight = jnp.exp2((scores[n] - largest) * EXP_SCALE)
            total = weight if total is None else total + weight
            one = jnp.dot(weight.astype(jnp.bfloat16), pairs[n](1), preferred_element_type=jnp.float32)
            acc = one if acc is None else acc + one
        totals = jnp.sum(total, axis=1, keepdims=True)
        target[...] = (acc / totals).astype(jnp.bfloat16)

    def attend_send(j):
        attend(j, ctx_out.at[j])
        go(ctx_out.at[j], ctx.at[me], send_ctx.at[j], recv_ctx.at[me], owner(j))

    def out_project():
        left = jnp.concatenate([ctx[h] for h in range(8)], axis=1)

        def body(n, _):
            zz, yy = div(n, 2), 2 * rem(n, 2)
            weights = jnp.concatenate(
                [wo[:, zz, yy].reshape(1024, 128), wo[:, zz, yy + 1].reshape(1024, 128)], axis=1)
            result = jnp.dot(left, weights, preferred_element_type=jnp.float32)
            out[:, pl.ds(pl.multiple_of(n * 256, 256), 256)] = result.astype(jnp.bfloat16)
            return 0

        lax.fori_loop(0, 8, body, 0)

    own, pal = me, slab(0, 1 - c)
    near = [slab(-sign, c), slab(sign, 1 - c), slab(sign, c), slab(-sign, 1 - c)]
    far = [slab(2, c), slab(2, 1 - c)]

    def handle(j):
        project_kv(j)
        halo_send(j)

    tok_start()
    for k in range(1, 8):
        go(masks.at[me], masks.at[me], send_mask.at[k], recv_mask.at[me], owner(rem(me + k, 8)))
    for p in (K, V, Q, O0, O1):
        first_start(p)
    for p in (K, V, Q):
        second_start(p)
    for p in (O0, O1):
        ring_relay(p, 0)
    for p in (O0, O1):
        second_start(p)
    tok_relay(0)
    for p in (K, V):
        ring_finish(p, 1, True)
    handle(own)
    tok_mate(0)
    handle(pal)
    for n in range(1, CHUNKS):
        tok_relay(n)
    for n in range(CHUNKS):
        tok_pass(n)
    for p in (O0, O1):
        second_relay(p)
    ring_finish(Q, 1, True)
    handle(near[0])
    handle(near[2])
    tok_mate(1)
    handle(near[1])
    tok_mate(2)
    handle(near[3])
    for p in (O0, O1):
        second_finish(p)
    for n in range(CHUNKS):
        tok_last(n)
    project_q(own)
    project_q(pal)
    for k in range(1, 8):
        j = rem(me + k, 8)
        arrived(masks.at[j], recv_mask.at[j])
    attend(own, ctx.at[me])
    attend_send(pal)
    handle(far[0])
    tok_mate(3)
    handle(far[1])
    for j in near:
        project_q(j)
    for j in near:
        attend_send(j)
    for j in far:
        project_q(j)
    for j in far:
        attend_send(j)
    for p in (O0, O1):
        from_mate(p)
    for k in range(1, 8):
        j = rem(me + k, 8)
        arrived(ctx.at[j], recv_ctx.at[j])
    out_project()
    for copy in sends:
        copy.wait_send()
    for pred, copy in conditional:
        @pl.when(pred)
        def _(copy=copy):
            copy.wait_send()


def per_device(tokens, w_qkv, w_out, neighbours, counts):
    dma = pltpu.SemaphoreType.DMA
    vmem, hbm = pl.BlockSpec(memory_space=pltpu.VMEM), pl.BlockSpec(memory_space=pl.ANY)
    bf16 = jnp.bfloat16
    return pl.pallas_call(
        kernel,
        out_shape=jax.ShapeDtypeStruct((256, 2048), bf16),
        in_specs=[hbm, hbm, hbm, vmem, vmem],
        out_specs=vmem,
        scratch_shapes=[
            pltpu.VMEM((3, 4, 4, 128, 128), bf16),
            pltpu.VMEM((8, 4, 4, 128, 128), bf16),
            pltpu.VMEM((256, 2048), bf16),
            pltpu.VMEM((8, 256, 2048), bf16),
            pltpu.VMEM((8, 256, 128), bf16),
            pltpu.VMEM((10, 2, 256, 128), bf16),
            pltpu.VMEM((8, 2, 256, 128), bf16),
            pltpu.VMEM((8, 2, 256, 128), bf16),
            pltpu.VMEM((8, 8, 256), jnp.float32),
            pltpu.VMEM((8, 256, 128), bf16),
            pltpu.VMEM((8, 256, 128), bf16),
            dma((7,)), dma,
            dma((5, 2, 3)), dma((5, 2, 3)),
            dma((2, 4)), dma((2, 4)),
            dma((3, CHUNKS)), dma((3, CHUNKS)),
            dma((4, CHUNKS)), dma((4, CHUNKS)),
            dma((8,)), dma((8,)),
            dma((8,)), dma((8,)), dma((8,)), dma((8,)),
            dma, dma,
            dma((8,)), dma((8,)),
        ],
        compiler_params=pltpu.CompilerParams(
            collective_id=0, has_side_effects=True, vmem_limit_bytes=60 << 20),
    )(tokens, w_qkv, w_out, neighbours, counts.reshape(1, 256))


def solution(mesh):
    placed = (P(("outer", "inner"), None), P("inner", None), P(None, "inner"), P(("outer", "inner"), None), P())
    return jax.shard_map(
        per_device, mesh=mesh, in_specs=placed, out_specs=P(("outer", "inner"), None), check_vma=False)
```

time: 285 us -> 84.6 us (0.30)
  the two profiles are of different devices: /device:TPU:152 before, /device:TPU:96 now
where the time goes in v2:
time: 84.6 us; the launch traced here: 84.5 us
  Pallas kernels  82.1 us (97%)
  local copies, waits for them, and re-layouts  2.3 us (3%)
    pallas_call x1, Pallas kernels, per_device(): pl.pallas_call(kernel, out_shape=jax.ShapeDtypeStruct((256, 2048), bf16),...  82.1 us
    unnamed x1, local copies, waits for them, and re-layouts  2.3 us

profile of v2, /device:TPU:96, one launch (start us, length us, event | category | flops | bytes accessed | tf_op | source)
XLA Modules:
  0.0 84.5 jit_solution(9476090331292319841)
XLA Ops:
  0.0 82.1 %shard_map.55 = bf16[256,2048]{1,0:T(8,128)(2,1)} custom-call(bf16[256,2048]{1,0:T(8,128)(2,1)} %tokens.1, bf16[128,3072]{1,0:T(8,128)(2,1)} %w_qkv.1, bf16[1024,128]{1,0:T(8,128)(2,1)} %w_out.1, s32[1,5]{1,0:T(1,128)} %listed.1, s32[1,256]{1,0:T(1,128)} %bitcast.1), custom_call_target="tpu_custom_call" | custom-call | tf_op jit(solution)/shard_map/pallas_call | solution.py:397
  82.1 2.3 %copy.7 = bf16[256,2048]{1,0:T(8,128)(2,1)} copy(bf16[256,2048]{1,0:T(8,128)(2,1)} %shard_map.55) | data formatting | bytes 2097152

commit v3 on v2

--- a/solution.py
+++ b/solution.py
@@ -11,14 +11,15 @@
 HD = 128
 EXP_SCALE = float(HD) ** (-0.5) * math.log2(math.e)
 Q, K, V, O0, O1 = 0, 1, 2, 3, 4
-Z_FIRST = {Q: True, K: True, V: False, O0: True, O1: False}
+Z_FIRST = {Q: True, K: True, V: False, O0: False, O1: False}
 CHUNKS = 2
 ROWS = 256 // CHUNKS
 
 
 def kernel(tokens, w_qkv, w_out, listed, counts, out, wh, wo, raw, normed, queries, kv, above, below, masks, ctx_out, ctx,
            load_sem, tok_sem, recv_ring, send_ring, recv_mate, send_mate, recv_tok, send_tok, recv_tmate, send_tmate,
-           recv_mask, send_mask, recv_up, recv_down, send_up, send_down, recv_edge, send_edge, recv_ctx, send_ctx):
+           recv_mask, send_mask, recv_up, recv_down, send_up, send_down, recv_edge, send_edge, recv_ctx, send_ctx,
+           edge_buf, cross_buf, recv_half, send_half, recv_cross, send_cross):
     o, i = lax.axis_index("outer"), lax.axis_index("inner")
     div, rem = lax.div, lax.rem
     x, c = rem(div(o, 2), 4), rem(o, 2)
@@ -39,6 +40,8 @@
     half, other = 4 * c, 4 * (1 - c)
     across_up = (y == 3) & (zl < 3)
     across_down = (y == 0) & (zl > 0)
+    turn_up, turn_down = (c == 1) & across_up, (c == 1) & across_down
+    corner_up, corner_down = (c == 1) & (y == 0) & (zl < 3), (c == 1) & (y == 3) & (zl > 0)
 
     tok_copy = pltpu.make_async_copy(tokens, raw, tok_sem)
     tok_copy.start()
@@ -63,7 +66,7 @@
 
     peers = [owner(rem(me + k, 8)) for k in range(1, 8)]
     peers += [dev(x, y, z + 1, c), dev(x, y, z - 1, c), dev(x, y + 1, z, c), dev(x, y - 1, z, c),
-              dev(x, y, z + 2, c), dev(x, y, z - 2, c), dev(x, y + 2, z, c), dev(x, y, z + 4, c)]
+              dev(x, y, z + 2, c), dev(x, y, z - 2, c), dev(x, y + 2, z, c)]
     for device in peers:
         greet(device)
 
@@ -193,7 +196,7 @@
 
     def second_start(p):
         ring_finish(p, 0, p < O0)
-        ring_start(p, 1, p < O0)
+        ring_start(p, 1)
         if p >= O0:
             to_mate(p, 0, part(p, 1, 0))
 
@@ -258,9 +261,30 @@
 
     def halo_send(j):
         ref = kv.at[j + 1]
-        when_go(i < 15, remote(ref, below.at[j], send_up.at[j], recv_down.at[j], up))
-        when_go(i > 0, remote(ref, above.at[j], send_down.at[j], recv_up.at[j], down))
-        when_go(j == edge_slab, remote(ref, kv.at[9 * zh], send_edge, recv_edge, dev(x, y, z + 4, c)))
+        when_go((i < 15) & jnp.logical_not(turn_up), remote(ref, below.at[j], send_up.at[j], recv_down.at[j], up))
+        when_go((i > 0) & jnp.logical_not(turn_down), remote(ref, above.at[j], send_down.at[j], recv_up.at[j], down))
+        when_go(turn_up, remote(ref, cross_buf.at[j], send_up.at[j], recv_cross.at[j], dev(x, y + 1, z, c)))
+        when_go(turn_down, remote(ref, cross_buf.at[j], send_down.at[j], recv_cross.at[j], dev(x, y - 1, z, c)))
+        when_go(j == edge_slab, remote(ref, edge_buf, send_half, recv_half, dev(x, y, z + 2 * sign, c)))
+
+    def cross_relay(j):
+        ref = cross_buf.at[j]
+
+        @pl.when(corner_up | corner_down)
+        def _():
+            arrived(ref, recv_cross.at[j])
+        when_go(corner_up, remote(ref, below.at[j], send_cross.at[j], recv_down.at[j], dev(x, y, z + 1, c)))
+        when_go(corner_down, remote(ref, above.at[j], send_cross.at[j], recv_up.at[j], dev(x, y, z - 1, c)))
+
+    end = rem(z + 2 * sign + 8, 8)
+
+    def edge_relay(pred):
+        @pl.when(pred)
+        def _():
+            arrived(edge_buf, recv_half)
+        when_go(pred, remote(edge_buf, kv.at[9 * (1 - div(end, 4))], send_edge, recv_edge, dev(x, y, end, c)))
+
+    outer_x = (x == 0) | (x == 3)
 
     def project_q(j):
         queries[j] = jnp.dot(normed[j], wh[Q].reshape(2048, 128), preferred_element_type=jnp.float32).astype(jnp.bfloat16)
@@ -333,21 +357,25 @@
         second_start(p)
     for p in (O0, O1):
         ring_relay(p, 0)
+    for p in (K, V, Q):
+        ring_relay(p, 1)
     for p in (O0, O1):
         second_start(p)
     tok_relay(0)
     for p in (K, V):
-        ring_finish(p, 1, True)
+        ring_finish(p, 1)
     handle(own)
     tok_mate(0)
     handle(pal)
     for n in range(1, CHUNKS):
         tok_relay(n)
+    cross_relay(own)
+    cross_relay(pal)
     for n in range(CHUNKS):
         tok_pass(n)
     for p in (O0, O1):
         second_relay(p)
-    ring_finish(Q, 1, True)
+    ring_finish(Q, 1)
     handle(near[0])
     handle(near[2])
     tok_mate(1)
@@ -356,18 +384,24 @@
     handle(near[3])
     for p in (O0, O1):
         second_finish(p)
+    project_q(own)
+    project_q(pal)
+    for j in (near[0], near[2], near[1], near[3]):
+        cross_relay(j)
+    edge_relay(outer_x)
     for n in range(CHUNKS):
         tok_last(n)
-    project_q(own)
-    project_q(pal)
     for k in range(1, 8):
         j = rem(me + k, 8)
         arrived(masks.at[j], recv_mask.at[j])
-    attend(own, ctx.at[me])
-    attend_send(pal)
     handle(far[0])
     tok_mate(3)
     handle(far[1])
+    attend(own, ctx.at[me])
+    attend_send(pal)
+    edge_relay(jnp.logical_not(outer_x))
+    for j in far:
+        cross_relay(j)
     for j in near:
         project_q(j)
     for j in near:
@@ -420,6 +454,10 @@
             dma((8,)), dma((8,)), dma((8,)), dma((8,)),
             dma, dma,
             dma((8,)), dma((8,)),
+            pltpu.VMEM((2, 256, 128), bf16),
+            pltpu.VMEM((8, 2, 256, 128), bf16),
+            dma, dma,
+            dma((8,)), dma((8,)),
         ],
         compiler_params=pltpu.CompilerParams(
             collective_id=0, has_side_effects=True, vmem_limit_bytes=60 << 20),

time: 84.6 us -> 77.9 us (0.921)
  the two profiles are of different devices: /device:TPU:96 before, /device:TPU:1 now
where the time goes in v3:
time: 77.9 us; the launch traced here: 77.7 us
  Pallas kernels  75.4 us (97%)
  local copies, waits for them, and re-layouts  2.3 us (3%)
    pallas_call x1, Pallas kernels, per_device(): pl.pallas_call(kernel, out_shape=jax.ShapeDtypeStruct((256, 2048), bf16),...  75.4 us
    unnamed x1, local copies, waits for them, and re-layouts  2.3 us

profile of v3, /device:TPU:1, one launch (start us, length us, event | category | flops | bytes accessed | tf_op | source)
XLA Modules:
  0.0 77.7 jit_solution(13272852057727224855)
XLA Ops:
  0.0 75.4 %shard_map.55 = bf16[256,2048]{1,0:T(8,128)(2,1)} custom-call(bf16[256,2048]{1,0:T(8,128)(2,1)} %tokens.1, bf16[128,3072]{1,0:T(8,128)(2,1)} %w_qkv.1, bf16[1024,128]{1,0:T(8,128)(2,1)} %w_out.1, s32[1,5]{1,0:T(1,128)} %listed.1, s32[1,256]{1,0:T(1,128)} %bitcast.1), custom_call_target="tpu_custom_call" | custom-call | tf_op jit(solution)/shard_map/pallas_call | solution.py:431
  75.4 2.3 %copy.7 = bf16[256,2048]{1,0:T(8,128)(2,1)} copy(bf16[256,2048]{1,0:T(8,128)(2,1)} %shard_map.55) | data formatting | bytes 2097152

commit v4 on v3

--- a/solution.py
+++ b/solution.py
@@ -19,7 +19,7 @@
 def kernel(tokens, w_qkv, w_out, listed, counts, out, wh, wo, raw, normed, queries, kv, above, below, masks, ctx_out, ctx,
            load_sem, tok_sem, recv_ring, send_ring, recv_mate, send_mate, recv_tok, send_tok, recv_tmate, send_tmate,
            recv_mask, send_mask, recv_up, recv_down, send_up, send_down, recv_edge, send_edge, recv_ctx, send_ctx,
-           edge_buf, cross_buf, recv_half, send_half, recv_cross, send_cross):
+           cross_buf, recv_cross, send_cross):
     o, i = lax.axis_index("outer"), lax.axis_index("inner")
     div, rem = lax.div, lax.rem
     x, c = rem(div(o, 2), 4), rem(o, 2)
@@ -66,7 +66,7 @@
 
     peers = [owner(rem(me + k, 8)) for k in range(1, 8)]
     peers += [dev(x, y, z + 1, c), dev(x, y, z - 1, c), dev(x, y + 1, z, c), dev(x, y - 1, z, c),
-              dev(x, y, z + 2, c), dev(x, y, z - 2, c), dev(x, y + 2, z, c)]
+              dev(x, y, z + 2, c), dev(x, y, z - 2, c), dev(x, y + 2, z, c), dev(x, y, z + 4, c)]
     for device in peers:
         greet(device)
 
@@ -265,7 +265,7 @@
         when_go((i > 0) & jnp.logical_not(turn_down), remote(ref, above.at[j], send_down.at[j], recv_up.at[j], down))
         when_go(turn_up, remote(ref, cross_buf.at[j], send_up.at[j], recv_cross.at[j], dev(x, y + 1, z, c)))
         when_go(turn_down, remote(ref, cross_buf.at[j], send_down.at[j], recv_cross.at[j], dev(x, y - 1, z, c)))
-        when_go(j == edge_slab, remote(ref, edge_buf, send_half, recv_half, dev(x, y, z + 2 * sign, c)))
+        when_go(j == edge_slab, remote(ref, kv.at[9 * zh], send_edge, recv_edge, dev(x, y, z + 4, c)))
 
     def cross_relay(j):
         ref = cross_buf.at[j]
@@ -275,16 +275,6 @@
             arrived(ref, recv_cross.at[j])
         when_go(corner_up, remote(ref, below.at[j], send_cross.at[j], recv_down.at[j], dev(x, y, z + 1, c)))
         when_go(corner_down, remote(ref, above.at[j], send_cross.at[j], recv_up.at[j], dev(x, y, z - 1, c)))
-
-    end = rem(z + 2 * sign + 8, 8)
-
-    def edge_relay(pred):
-        @pl.when(pred)
-        def _():
-            arrived(edge_buf, recv_half)
-        when_go(pred, remote(edge_buf, kv.at[9 * (1 - div(end, 4))], send_edge, recv_edge, dev(x, y, end, c)))
-
-    outer_x = (x == 0) | (x == 3)
 
     def project_q(j):
         queries[j] = jnp.dot(normed[j], wh[Q].reshape(2048, 128), preferred_element_type=jnp.float32).astype(jnp.bfloat16)
@@ -388,7 +378,6 @@
     project_q(pal)
     for j in (near[0], near[2], near[1], near[3]):
         cross_relay(j)
-    edge_relay(outer_x)
     for n in range(CHUNKS):
         tok_last(n)
     for k in range(1, 8):
@@ -399,7 +388,6 @@
     handle(far[1])
     attend(own, ctx.at[me])
     attend_send(pal)
-    edge_relay(jnp.logical_not(outer_x))
     for j in far:
         cross_relay(j)
     for j in near:
@@ -454,9 +442,7 @@
             dma((8,)), dma((8,)), dma((8,)), dma((8,)),
             dma, dma,
             dma((8,)), dma((8,)),
-            pltpu.VMEM((2, 256, 128), bf16),
             pltpu.VMEM((8, 2, 256, 128), bf16),
-            dma, dma,
             dma((8,)), dma((8,)),
         ],
         compiler_params=pltpu.CompilerParams(

time: 77.9 us -> 77.2 us (level)
  no operation moved by 1% of the time
where the time goes in v4:
time: 77.2 us; the launch traced here: 77.1 us
  Pallas kernels  74.8 us (97%)
  local copies, waits for them, and re-layouts  2.3 us (3%)
    pallas_call x1, Pallas kernels, per_device(): pl.pallas_call(kernel, out_shape=jax.ShapeDtypeStruct((256, 2048), bf16),...  74.8 us
    unnamed x1, local copies, waits for them, and re-layouts  2.3 us

profile of v4, /device:TPU:1, one launch (start us, length us, event | category | flops | bytes accessed | tf_op | source)
XLA Modules:
  0.0 77.1 jit_solution(12343868034174730925)
XLA Ops:
  0.0 74.8 %shard_map.55 = bf16[256,2048]{1,0:T(8,128)(2,1)} custom-call(bf16[256,2048]{1,0:T(8,128)(2,1)} %tokens.1, bf16[128,3072]{1,0:T(8,128)(2,1)} %w_qkv.1, bf16[1024,128]{1,0:T(8,128)(2,1)} %w_out.1, s32[1,5]{1,0:T(1,128)} %listed.1, s32[1,256]{1,0:T(1,128)} %bitcast.1), custom_call_target="tpu_custom_call" | custom-call | tf_op jit(solution)/shard_map/pallas_call | solution.py:419
  74.8 2.3 %copy.7 = bf16[256,2048]{1,0:T(8,128)(2,1)} copy(bf16[256,2048]{1,0:T(8,128)(2,1)} %shard_map.55) | data formatting | bytes 2097152

commit v5 on v3

--- a/solution.py
+++ b/solution.py
@@ -66,7 +66,7 @@
 
     peers = [owner(rem(me + k, 8)) for k in range(1, 8)]
     peers += [dev(x, y, z + 1, c), dev(x, y, z - 1, c), dev(x, y + 1, z, c), dev(x, y - 1, z, c),
-              dev(x, y, z + 2, c), dev(x, y, z - 2, c), dev(x, y + 2, z, c)]
+              dev(x, y, z + 2, c), dev(x, y, z - 2, c), dev(x, y + 2, z, c), dev(x, y, z + 4, c)]
     for device in peers:
         greet(device)
 
@@ -215,22 +215,27 @@
         return 2 * rem(x + step + 4, 4) + core
 
     def tok_start():
-        for n in range(CHUNKS):
-            ref = rows_of(me, n)
-            go(ref, ref, send_tok.at[0, n], recv_tok.at[0, n], dev(x + 1, y, z, c))
-            go(ref, ref, send_tok.at[1, n], recv_tok.at[1, n], dev(x - 1, y, z, c))
+        evens, odds = list(range(0, CHUNKS, 2)), list(range(1, CHUNKS, 2))
+        for n, m in zip(evens + odds, odds + evens):
+            ref, back = rows_of(me, n), rows_of(me, m)
+            go(ref, ref, send_tok.at[c, n], recv_tok.at[c, n], dev(x + sign, y, z, c))
+            go(back, back, send_tok.at[1 - c, m], recv_tok.at[1 - c, m], dev(x - sign, y, z, c))
             go(ref, ref, send_tmate.at[0, n], recv_tmate.at[0, n], mate)
 
     def tok_relay(n):
-        ref = rows_of(slab(-sign, c), n)
-        arrived(ref, recv_tok.at[c, n])
-        go(ref, ref, send_tok.at[2, n], recv_tok.at[2, n], dev(x + sign, y, z, c))
-        go(ref, ref, send_tmate.at[1, n], recv_tmate.at[1, n], mate)
+        odd = n % 2
+        way = -sign if odd else sign
+        ref = rows_of(slab(-way, c), n)
+        arrived(ref, recv_tok.at[1 - c if odd else c, n])
+        go(ref, ref, send_tok.at[2, n], recv_tok.at[2, n], dev(x + way, y, z, c))
+        go(ref, ref, send_tmate.at[1 + odd, n], recv_tmate.at[1 + odd, n], mate)
 
     def tok_pass(n):
-        ref = rows_of(slab(sign, c), n)
-        arrived(ref, recv_tok.at[1 - c, n])
-        go(ref, ref, send_tmate.at[2, n], recv_tmate.at[2, n], mate)
+        odd = n % 2
+        way = -sign if odd else sign
+        ref = rows_of(slab(way, c), n)
+        arrived(ref, recv_tok.at[c if odd else 1 - c, n])
+        go(ref, ref, send_tmate.at[2 - odd, n], recv_tmate.at[2 - odd, n], mate)
 
     def tok_last(n):
         ref = rows_of(slab(2, c), n)
@@ -265,7 +270,7 @@
         when_go((i > 0) & jnp.logical_not(turn_down), remote(ref, above.at[j], send_down.at[j], recv_up.at[j], down))
         when_go(turn_up, remote(ref, cross_buf.at[j], send_up.at[j], recv_cross.at[j], dev(x, y + 1, z, c)))
         when_go(turn_down, remote(ref, cross_buf.at[j], send_down.at[j], recv_cross.at[j], dev(x, y - 1, z, c)))
-        when_go(j == edge_slab, remote(ref, edge_buf, send_half, recv_half, dev(x, y, z + 2 * sign, c)))
+        when_go(j == edge_slab, remote(ref, kv.at[9 * zh], send_edge, recv_edge, dev(x, y, z + 4, c)))
 
     def cross_relay(j):
         ref = cross_buf.at[j]
@@ -388,7 +393,6 @@
     project_q(pal)
     for j in (near[0], near[2], near[1], near[3]):
         cross_relay(j)
-    edge_relay(outer_x)
     for n in range(CHUNKS):
         tok_last(n)
     for k in range(1, 8):
@@ -399,7 +403,6 @@
     handle(far[1])
     attend(own, ctx.at[me])
     attend_send(pal)
-    edge_relay(jnp.logical_not(outer_x))
     for j in far:
         cross_relay(j)
     for j in near:

time: 77.9 us -> 77.2 us (level)
  no operation moved by 1% of the time
where the time goes in v5:
time: 77.2 us; the launch traced here: 77.1 us
  Pallas kernels  74.8 us (97%)
  local copies, waits for them, and re-layouts  2.3 us (3%)
    pallas_call x1, Pallas kernels, per_device(): pl.pallas_call(kernel, out_shape=jax.ShapeDtypeStruct((256, 2048), bf16),...  74.8 us
    unnamed x1, local copies, waits for them, and re-layouts  2.3 us

profile of v5, /device:TPU:1, one launch (start us, length us, event | category | flops | bytes accessed | tf_op | source)
XLA Modules:
  0.0 77.1 jit_solution(9826137337697601847)
XLA Ops:
  0.0 74.8 %shard_map.55 = bf16[256,2048]{1,0:T(8,128)(2,1)} custom-call(bf16[256,2048]{1,0:T(8,128)(2,1)} %tokens.1, bf16[128,3072]{1,0:T(8,128)(2,1)} %w_qkv.1, bf16[1024,128]{1,0:T(8,128)(2,1)} %w_out.1, s32[1,5]{1,0:T(1,128)} %listed.1, s32[1,256]{1,0:T(1,128)} %bitcast.1), custom_call_target="tpu_custom_call" | custom-call | tf_op jit(solution)/shard_map/pallas_call | solution.py:434
  74.8 2.3 %copy.7 = bf16[256,2048]{1,0:T(8,128)(2,1)} copy(bf16[256,2048]{1,0:T(8,128)(2,1)} %shard_map.55) | data formatting | bytes 2097152
